TPU v7x, 32 devices: a whole 2x2x4 slice. The times are simulated.
32 devices in a mesh: group: 2 (over x), lon: 8 (over z, y), lat: 2 (over core).
Axes of the slice: x: 2, y: 2, z: 4, core: 2. Of those that a mesh axis runs over, the one named last changes fastest.
Arguments:
- tokens: bfloat16 [128, 256, 384], P(('group', 'lat'), 'lon'), parts along dimension 0, may hold values from -6 to 6
- visible: int32 [128, 256], P(('group', 'lat'), 'lon'), parts along dimension 0, may hold values 0 or 1
- mask_token: bfloat16 [384], replicated, may hold values from -4 to 4
- norm_gain_table: float32 [2, 384], replicated, may hold values from 0.25 to 1.75
- query_key_value_weight: bfloat16 [2, 384, 1152], replicated, may hold values from -0.3125 to 0.3125
- output_weight: bfloat16 [2, 384, 384], replicated, may hold values from -0.3125 to 0.3125
- cotangent: float32 [128, 256, 384], P(('group', 'lat'), 'lon'), parts along dimension 0, may hold values from -6 to 6
Outputs:
- grad_tokens: float32 [128, 256, 384], P(('group', 'lat'), 'lon'), parts along dimension 0
- grad_qkv: float32 [4, 384, 1152], P('group'), parts along dimension 0
- grad_out: float32 [4, 384, 384], P('group'), parts along dimension 0
- grad_gain: float32 [4, 384], P('group'), parts along dimension 0
There are 2 independent parts, one for each index of `group`. A program takes and returns all parts, laid end to end along the dimension named above; an argument that names none is the same for every part. Nothing has to cross between parts.
Inputs may be any that keep to these rules, and one draw needn't show every extreme that they name: 1 marks a visible token.
All inputs are finite; a program needn't handle non-finite values. No bound on the sum of `visible` on one device may be relied on, other than what follows from the above.
Results may differ from a plain program's by a relative error of at most 0.01.
Values may be sent and summed in bfloat16 or wider, within the bound.
No kernel may reach another device: no remote copies, remote signals or barrier semaphores. Data moves between devices by JAX's collectives and lax.ppermute only.
A program may use at most 320 MiB of HBM per device.

v0:
```python
import jax
import jax.numpy as jnp
from jax import lax
from jax.sharding import PartitionSpec as P

HEADS = 6


def partner(value, axis, stride):
    mask = 2**stride
    pairs = [(source, source ^ mask) for source in range(lax.axis_size(axis))]
    return lax.ppermute(value, axis, pairs)


def passed_along(value, axis, steps):
    count = lax.axis_size(axis)
    pairs = [(source, (source + steps) % count) for source in range(count)]
    return lax.ppermute(value, axis, pairs)


def extended_2(cells, sides, width):
    for axis, dim in sides:
        count = lax.axis_size(axis)
        head = lax.slice_in_dim(cells, 0, width, axis=dim)
        tail = lax.slice_in_dim(cells, cells.shape[dim] - width, cells.shape[dim], axis=dim)
        cells = jnp.concatenate(
            [
                lax.ppermute(tail, axis, [(i, (i + 1) % count) for i in range(count)]),
                cells,
                lax.ppermute(head, axis, [((i + 1) % count, i) for i in range(count)]),
            ],
            axis=dim,
        )
    return cells


def normed(values_in, gain_row):
    mean_value = jnp.mean(values_in, axis=-1, keepdims=True)
    centred = values_in - mean_value
    spread = jnp.mean(centred * centred, axis=-1, keepdims=True)
    return centred * lax.rsqrt(spread + 1e-05) * gain_row


def mix_heads(query_heads, key_list, value_list, mask_list):
    head_size = query_heads.shape[1]
    weights = []
    for key_one, mask_one in zip(key_list, mask_list):
        weight_one = jnp.exp(jnp.sum(query_heads * key_one, axis=1) * head_size ** (-0.5))
        if mask_one is not None:
            weight_one = weight_one * mask_one
        weights.append(weight_one)
    weight_sum = sum(weights)
    result = jnp.zeros_like(query_heads)
    for weight_one, value_one in zip(weights, value_list):
        result = result + (weight_one / weight_sum)[:, None, :] * value_one
    return result


def dilated_mix(query_flat, blocks):
    width = query_flat.shape[0]
    head_size = width // HEADS
    points = query_flat.shape[1]
    query_heads = query_flat.reshape(HEADS, head_size, points)
    key_list = [
        blocks[number, :width].reshape(HEADS, head_size, points)
        for number in range(blocks.shape[0])
    ]
    value_list = [
        blocks[number, width:].reshape(HEADS, head_size, points)
        for number in range(blocks.shape[0])
    ]
    mask_list = [None for number in range(blocks.shape[0])]
    return mix_heads(query_heads, key_list, value_list, mask_list).reshape(width, points)


def plain_mix(query_grid, padded, lat_masks, grid_rows, grid_cols, margin):
    width = query_grid.shape[0]
    head_size = width // HEADS
    points = grid_rows * grid_cols
    placed = jnp.pad(query_grid, ((0, 0), (1, 1), (1, 1))).reshape(HEADS, head_size, points)
    key_list = []
    value_list = []
    mask_list = []
    for lat_step in (-1, 0, 1):
        for lon_step in (-1, 0, 1):
            start_at = margin + lat_step * grid_cols + lon_step
            window = padded[:, start_at : start_at + points]
            key_list.append(window[:width].reshape(HEADS, head_size, points))
            value_list.append(window[width:].reshape(HEADS, head_size, points))
            mask_list.append(lat_masks[lat_step + 1])
    result = mix_heads(placed, key_list, value_list, mask_list).reshape(width, grid_rows, grid_cols)
    return result[:, 1 : grid_rows - 1, 1 : grid_cols - 1]


def surround(block_in):
    partner_block = partner(block_in, "lat", 0)
    pair_blocks = jnp.stack([block_in, partner_block])
    moved_blocks = [passed_along(pair_blocks, "lon", step_dir) for step_dir in (1, -1)]
    return jnp.concatenate([pair_blocks, moved_blocks[0], moved_blocks[1]], 0)


def gather_back(grad_blocks):
    pair_blocks = grad_blocks[0:2]
    for step_dir, rim_part in ((-1, grad_blocks[2:4]), (1, grad_blocks[4:6])):
        pair_blocks = pair_blocks + passed_along(
            rim_part.astype(jnp.bfloat16), "lon", step_dir
        ).astype(rim_part.dtype)
    return pair_blocks[0] + partner(pair_blocks[1].astype(jnp.bfloat16), "lat", 0).astype(
        jnp.float32
    )


def widen_plain(keyval_grid):
    row_count = keyval_grid.shape[1]
    is_upper = lax.axis_index("lat") == 0
    outgoing = jnp.where(is_upper, keyval_grid[:, row_count - 1 :], keyval_grid[:, :1])
    partner_row = partner(outgoing, "lat", 0)
    empty_row = jnp.zeros_like(partner_row)
    lat_band = jnp.where(
        is_upper,
        jnp.concatenate([empty_row, keyval_grid, partner_row], 1),
        jnp.concatenate([partner_row, keyval_grid, empty_row], 1),
    )
    return extended_2(lat_band, (("lon", 2),), 1)


def fold_plain(grad_grid):
    grid_rows = grad_grid.shape[1]
    grid_cols = grad_grid.shape[2]
    col_count = grid_cols - 2
    row_count = grid_rows - 2
    core_part = grad_grid[:, :, 1 : grid_cols - 1]
    for step_dir, rim_part in ((-1, grad_grid[:, :, :1]), (1, grad_grid[:, :, grid_cols - 1 :])):
        arrived = passed_along(rim_part.astype(jnp.bfloat16), "lon", step_dir).astype(
            rim_part.dtype
        )
        before = col_count - 1 if step_dir == -1 else 0
        core_part = core_part + jnp.pad(arrived, ((0, 0), (0, 0), (before, col_count - 1 - before)))
    is_upper = lax.axis_index("lat") == 0
    outgoing = jnp.where(is_upper, core_part[:, grid_rows - 1 :], core_part[:, :1])
    returned = partner(outgoing.astype(jnp.bfloat16), "lat", 0).astype(outgoing.dtype)
    own_part = core_part[:, 1 : grid_rows - 1]
    placed = jnp.where(
        is_upper,
        jnp.pad(returned, ((0, 0), (row_count - 1, 0), (0, 0))),
        jnp.pad(returned, ((0, 0), (0, row_count - 1), (0, 0))),
    )
    return own_part + placed


def project_features(normal_flat, weight_part):
    return jnp.einsum(
        "nd,de->en", normal_flat, weight_part, preferred_element_type=jnp.float32
    ).astype(jnp.bfloat16)


def forward_layer(layer_in, gain_row, weight_qkv, weight_out, dilated):
    row_count, col_count, width = layer_in.shape
    points = row_count * col_count
    normal_part, norm_pull = jax.vjp(normed, layer_in, gain_row)
    normal_half = normal_part.astype(jnp.bfloat16).reshape(points, width)
    query_flat = project_features(normal_half, weight_qkv[:, :width])
    grid_info = None
    if dilated:
        wide_input = normal_half
        blocks = surround(project_features(normal_half, weight_qkv[:, width:]))
        mixed_flat, attend_pull = jax.vjp(
            dilated_mix, query_flat.astype(jnp.float32), blocks.astype(jnp.float32)
        )
    else:
        wide_input = normal_half
        keyval_grid = project_features(normal_half, weight_qkv[:, width:]).reshape(
            2 * width, row_count, col_count
        )
        extended = widen_plain(keyval_grid)
        grid_rows = row_count + 2
        grid_cols = col_count + 2
        margin = grid_cols + 1
        grid_points = grid_rows * grid_cols
        padded = jnp.pad(extended.reshape(2 * width, grid_points), ((0, 0), (margin, margin)))
        row_index = jnp.arange(grid_points, dtype=jnp.int32) // grid_cols
        outside_row = jnp.where(lax.axis_index("lat") == 0, 0, grid_rows - 1)
        lat_masks = []
        for lat_step in (-1, 0, 1):
            target = row_index + lat_step
            lat_masks.append(
                jnp.where(
                    (target >= 0) & (target <= grid_rows - 1) & (target != outside_row), 1.0, 0.0
                ).astype(jnp.float32)
            )

        def local_mix(query_grid, padded_in):
            return plain_mix(query_grid, padded_in, lat_masks, grid_rows, grid_cols, margin)

        query_grid = query_flat.astype(jnp.float32).reshape(width, row_count, col_count)
        mixed_grid, attend_pull = jax.vjp(local_mix, query_grid, padded.astype(jnp.float32))
        mixed_flat = mixed_grid.reshape(width, points)
        grid_info = (grid_rows, grid_cols, margin)
    mixed_half = mixed_flat.astype(jnp.bfloat16)
    layer_out = layer_in.reshape(points, width) + jnp.einsum(
        "dn,de->ne", mixed_half, weight_out, preferred_element_type=jnp.float32
    )
    saved = (
        norm_pull,
        attend_pull,
        normal_half,
        wide_input,
        mixed_half,
        dilated,
        grid_info,
        (row_count, col_count),
    )
    return (layer_out.reshape(row_count, col_count, width), saved)


def backward_layer(grad_in, saved, weight_qkv, weight_out):
    norm_pull, attend_pull, normal_half, wide_input, mixed_half, dilated, grid_info, shape_info = (
        saved
    )
    row_count, col_count = shape_info
    points, width = normal_half.shape
    highest = lax.Precision.HIGHEST
    weight_full = weight_qkv.astype(jnp.float32)
    normal_full = normal_half.astype(jnp.float32)
    grad_mixed = jnp.einsum("ne,de->dn", grad_in, weight_out.astype(jnp.float32), precision=highest)
    grad_wout = jnp.einsum("dn,ne->de", mixed_half.astype(jnp.float32), grad_in, precision=highest)
    if dilated:
        grad_query, grad_blocks = attend_pull(grad_mixed)
    else:
        grad_query_grid, grad_padded = attend_pull(grad_mixed.reshape(width, row_count, col_count))
        grad_query = grad_query_grid.reshape(width, points)
        grid_rows, grid_cols, margin = grid_info
        grad_grid = grad_padded[:, margin : margin + grid_rows * grid_cols].reshape(
            2 * width, grid_rows, grid_cols
        )
        grad_blocks = fold_plain(grad_grid).reshape(2 * width, points)
    grad_normal = jnp.einsum("en,de->nd", grad_query, weight_full[:, :width], precision=highest)
    grad_wquery = jnp.einsum("nd,en->de", normal_full, grad_query, precision=highest)
    grad_kvown = gather_back(grad_blocks) if dilated else grad_blocks
    grad_wkv = jnp.einsum("nd,en->de", normal_full, grad_kvown, precision=highest)
    grad_normal = grad_normal + jnp.einsum(
        "en,de->nd", grad_kvown, weight_full[:, width:], precision=highest
    )
    grad_field, grad_gain = norm_pull(grad_normal.reshape(row_count, col_count, width))
    return (
        grad_in + grad_field.reshape(points, width),
        jnp.concatenate([grad_wquery, grad_wkv], axis=1),
        grad_wout,
        grad_gain,
    )


def local(
    tokens, visible, mask_token, norm_gain_table, query_key_value_weight, output_weight, cotangent
):
    row_count, col_count, width = tokens.shape
    lat_count = lax.axis_size("lat")
    lon_count = lax.axis_size("lon")
    shown = visible[..., None] == 1
    starting_tokens = jnp.where(
        shown, tokens.astype(jnp.float32), mask_token.astype(jnp.float32)[None, None, :]
    )
    between_tokens, saved_first = forward_layer(
        starting_tokens, norm_gain_table[0], query_key_value_weight[0], output_weight[0], True
    )
    middle_half = lax.optimization_barrier(between_tokens.astype(jnp.bfloat16)).astype(jnp.float32)
    unused_final, saved_second = forward_layer(
        middle_half, norm_gain_table[1], query_key_value_weight[1], output_weight[1], False
    )
    grad_final = cotangent.reshape(row_count * col_count, width)
    gradient_between, qkv_second, out_second, gain_second = backward_layer(
        grad_final, saved_second, query_key_value_weight[1], output_weight[1]
    )
    grad_start, qkv_first, out_first, gain_first = backward_layer(
        gradient_between, saved_first, query_key_value_weight[0], output_weight[0]
    )
    grad_tokens = jnp.where(shown, grad_start.reshape(row_count, col_count, width), 0.0)
    summed_qkv, summed_out, summed_gain = lax.psum(
        (
            jnp.stack([qkv_first, qkv_second]),
            jnp.stack([out_first, out_second]),
            jnp.stack([gain_first, gain_second]),
        ),
        ("lon", "lat"),
    )
    factor = (row_count * col_count * lat_count * lon_count) ** (-0.5)
    return (grad_tokens, summed_qkv * factor, summed_out * factor, summed_gain * factor)


def solution(mesh):
    return jax.shard_map(
        local,
        mesh=mesh,
        in_specs=(
            P(("group", "lat"), "lon", None),
            P(("group", "lat"), "lon"),
            P(),
            P(),
            P(),
            P(),
            P(("group", "lat"), "lon", None),
        ),
        out_specs=(
            P(("group", "lat"), "lon", None),
            P("group", None, None),
            P("group", None, None),
            P("group", None),
        ),
        check_vma=False,
    )
```

profile of v0, /device:TPU:0, one launch (start us, length us, event | category | flops | bytes accessed | tf_op | source)
XLA Modules:
  0.0 959.3 jit_solution(4182502671617775337)
XLA Ops:
  43.2 119.3 %collective-permute-done.1 = bf16[2,768,1024]{2,1,0:T(8,128)(2,1)} collective-permute-done((bf16[2,768,1024]{2,1,0:T(8,128)(2,1)}, bf16[2,768,1024]{2,1,0:T(8,128)(2,1)}, u32[]{:S(2)}, u32[]{:S(2)}) %collective-permute-start.1) | collective-permute-done | bytes 3145760 | tf_op jit(solution)/shard_map/ppermute | solution.py:18
  170.0 6.6 fusion.90
  176.6 5.4 copy-done
  182.1 6.0 multiply_reduce_fusion.26
  213.8 10.1 %fusion.92 = (f32[384,1156]{0,1:T(8,128)}, f32[384,1156]{0,1:T(8,128)}, f32[384,1156]{0,1:T(8,128)}, f32[384,1156]{0,1:T(8,128)}, f32[384,1156]{0,1:T(8,128)}, /...) fusion(f32[768,1226]{0,1:T(8,128)S(1)} %pad_convert_fusion), kind=kLoop, calls=%fused_computation.281 | loop fusion | bytes 63922176 | tf_op jit(solution)/shard_map/jvp()/slice | solution.py:88
  290.0 24.3 %multiply_reduce_fusion.17 = (f32[6,1156]{0,1:T(8,128)}, f32[6,1156]{0,1:T(8,128)S(1)}, f32[6,1156]{0,1:T(8,128)S(1)}, f32[6,1156]{0,1:T(8,128)}, f32[6,1156]{0,...) fusion(f32[6,64,1156]{1,0,2:T(8,128)} %reshape.1855, ...), kind=kLoop, calls=%fused_computation.21 | loop fusion | flops 7927848 | bytes 18005856 | tf_op jit(solution)/shard_map/transpose(jvp())/reduce_sum | solution.py:55
  391.4 24.1 %multiply_reduce_fusion.16 = (f32[6,1156]{0,1:T(8,128)}, f32[6,1156]{0,1:T(8,128)S(1)}, f32[6,1156]{0,1:T(8,128)S(1)}, f32[6,1156]{0,1:T(8,128)}, f32[6,1156]{0,...) fusion(f32[6,64,1156]{1,0,2:T(8,128)} %reshape.1864, ...), kind=kLoop, calls=%fused_computation.20 | loop fusion | flops 7927848 | bytes 18005856 | tf_op jit(solution)/shard_map/jvp()/reduce_sum | solution.py:48
  466.1 5.6 bitcast_multiply_fusion.29
  493.1 9.4 pad_add_fusion.13
  502.5 10.4 %pad_add_fusion.1 = f32[768,1156]{1,0:T(8,128)} fusion(f32[768,1156]{1,0:T(8,128)} %pad_add_fusion.7, f32[768,1156]{1,0:T(8,128)S(1)} %pad_add_fusion.8, f32[768,1156]{1,0:T(8,128)S(1)} %pad_add_fusion.9, f32[768,1156]{1,0:T(8,128)S(1)} %pad_add_fusion.10, f32[768,1156]{1,0:T(8,128)S(1)} %pad_add_fusion.11, f32[768,1156]{1,0:T(8,128)S(1)} %pad_add_fusion.12, ...), kind=kLoop, calls=%fused_computation.22 | loop fusion | flops 5326848 | bytes 28409856 | tf_op jit(solution)/shard_map/transpose(jvp())/add_any | solution.py:87
  512.9 5.3 copy.367
  541.2 5.2 broadcast_in_dim.186
  568.9 5.2 broadcast_in_dim.190
  587.4 5.2 broadcast_in_dim.194
  606.2 5.2 broadcast_in_dim.198
  642.5 9.2 bitcast_multiply_fusion.10
  651.8 12.2 %fusion.89 = (bf16[6,768,1024]{2,1,0:T(8,128)(2,1)S(1)}, f32[6,768,1024]{2,1,0:T(8,128)}) fusion(f32[1,384,1024]{2,1,0:T(8,128)} %bitcast.394, f32[1,384,1024]{2,1,0:T(8,128)} %bitcast.395, f32[1,384,1024]{2,1,0:T(8,128)} %bitcast.396, f32[1,384,1024]{2,1,0:T(8,128)} %bitcast.397, f32[1,384,1024]{2,1,0:T(8,128)} %bitcast.398, ...), kind=kLoop, calls=%fused_computation.278 | loop fusion | flops 56623104 | bytes 47185920 | tf_op jit(solution)/shard_map/convert.12
  727.3 5.2 mul.2013
  782.8 5.6 mul.2027
  800.9 9.7 %convolution_bitcast_fusion.1 = f32[1,384,384]{2,1,0:T(8,128)S(1)} fusion(f32[32,32,384]{2,1,0:T(8,128)S(1)} %copy-done.15, f32[384,34,34]{0,2,1:T(8,128)} %reshape.1907, f32[384,34,34]{0,2,1:T(8,128)} %mul.2027, f32[384,34,34]{0,2,1:T(8,128)} %reshape.1906, f32[384,34,34]{0,2,1:T(8,128)} %mul.2025, f32[384,34,34]{0,2,1:T(8,128)} %reshape.1905, ...), kind=kOutput, calls=%fused_computation.162 | convolution fusion | flops 1815871488 | bytes 17891328 | tf_op jit(solution)/shard_map/dn,ne->de/dot_general | solution.py:226
  812.1 6.3 fusion
  833.2 7.4 fusion.5
  846.7 30.4 %psum.23 = f32[2,384]{1,0:T(2,128)S(1)} all-reduce(f32[2,384]{1,0:T(2,128)S(1)} %pad_maximum_fusion.4), channel_id=1, replica_groups=mesh['group'=2,'lon'=8,'lat'=2] {'lon','lat'}, use_global_device_ids=true, to_apply=%region_42.43 | all-reduce | flops 768 | bytes 6144 | tf_op jit(solution)/shard_map/psum | solution.py:278
  880.6 66.4 %all-reduce.49.cloned.1.call-done = (f32[2,384,1152]{2,1,0:T(8,128)}, f32[2,384,384]{2,1,0:T(8,128)}) async-done(((f32[2,384,1152]{2,1,0:T(8,128)}, f32[2,384,384]{2,1,0:T(8,128)}), (f32[2,384,1152]{2,1,0:T(8,128)}, f32[2,384,384]{2,1,0:T(8,128)})) %all-reduce.49.cloned.1.call-update) | async-done | bytes 4718608 | tf_op jit(solution)/shard_map/psum | solution.py:278
  (603 shorter events, 543.4 us)
Async XLA Ops:
  7.2 939.8 %all-reduce.49.cloned.1.call-start = ((), (), s32[]{:S(2)}) async-start(), calls=%async_computation | async-start | bytes 9437184 | tf_op jit(solution)/shard_map/psum | solution.py:278
  13.3 178.8 %copy-start.176 = (f32[384]{0:T(512)}, f32[384]{0:T(512)S(1)}, u32[]{:S(2)}) copy-start(f32[384]{0:T(512)S(1)} %get-tuple-element.38) | copy-start | bytes 4612
  17.2 22.9 %copy-start.36 = (bf16[32,32,384]{2,1,0:T(8,128)(2,1)}, bf16[32,32,384]{2,1,0:T(8,128)(2,1)S(1)}, u32[]{:S(2)}) copy-start(bf16[32,32,384]{2,1,0:T(8,128)(2,1)S(1)} %get-tuple-element.114) | copy-start | bytes 2359300
  18.3 3.5 collective-permute-start
  24.2 138.3 %collective-permute-start.1 = (bf16[2,768,1024]{2,1,0:T(8,128)(2,1)}, bf16[2,768,1024]{2,1,0:T(8,128)(2,1)}, u32[]{:S(2)}, u32[]{:S(2)}) collective-permute-start(bf16[2,768,1024]{2,1,0:T(8,128)(2,1)} %pad_maximum_fusion.1), channel_id=1, source_target_pairs={{0,2},{2,4},{4,6},{6,8},{8,10},{10,12},{12,14},{14,0},{1,3},{3,5},... | collective-permute-start | bytes 9437192 | tf_op jit(solution)/shard_map/ppermute | solution.py:18
  27.1 138.1 %collective-permute-start.2 = (bf16[2,768,1024]{2,1,0:T(8,128)(2,1)}, bf16[2,768,1024]{2,1,0:T(8,128)(2,1)}, u32[]{:S(2)}, u32[]{:S(2)}) collective-permute-start(bf16[2,768,1024]{2,1,0:T(8,128)(2,1)} %pad_maximum_fusion.1), channel_id=1, source_target_pairs={{0,14},{2,0},{4,2},{6,4},{8,6},{10,8},{12,10},{14,12},{1,15},{3,1}... | collective-permute-start | bytes 9437192 | tf_op jit(solution)/shard_map/ppermute | solution.py:18
  193.7 1.3 collective-permute-start.3
  195.4 12.1 %collective-permute-start.4 = (bf16[768,34,1]{0,2,1:T(2,128)(2,1)S(1)}, bf16[768,34,1]{0,2,1:T(2,128)(2,1)S(1)}, u32[]{:S(2)}, u32[]{:S(2)}) collective-permute-start(bf16[768,34,1]{0,2,1:T(2,128)(2,1)S(1)} %get-tuple-element.106), channel_id=1, source_target_pairs={{0,2},{2,4},{4,6},{6,8},{8,10},{10,12},{12,14},{14,0},{1,3},{3,5},... | collective-permute-start | bytes 156680 | tf_op jit(solution)/shard_map/ppermute | solution.py:28
  195.5 12.1 %collective-permute-start.5 = (bf16[768,34,1]{0,2,1:T(2,128)(2,1)S(1)}, bf16[768,34,1]{0,2,1:T(2,128)(2,1)S(1)}, u32[]{:S(2)}, u32[]{:S(2)}) collective-permute-start(bf16[768,34,1]{0,2,1:T(2,128)(2,1)S(1)} %get-tuple-element.107), channel_id=1, source_target_pairs={{2,0},{4,2},{6,4},{8,6},{10,8},{12,10},{14,12},{0,14},{3,1},{5,3},... | collective-permute-start | bytes 156680 | tf_op jit(solution)/shard_map/ppermute | solution.py:30
  317.4 109.0 %copy-start.131 = (f32[6,1156]{1,0:T(8,128)}, f32[6,1156]{1,0:T(8,128)S(1)}, u32[]{:S(2)}) copy-start(f32[6,1156]{1,0:T(8,128)S(1)} %copy.292) | copy-start | bytes 83236
  318.8 107.7 %copy-start.132 = (f32[6,1156]{1,0:T(8,128)}, f32[6,1156]{1,0:T(8,128)S(1)}, u32[]{:S(2)}) copy-start(f32[6,1156]{1,0:T(8,128)S(1)} %copy.295) | copy-start | bytes 83236
  325.2 101.3 %copy-start.133 = (f32[6,1156]{1,0:T(8,128)}, f32[6,1156]{1,0:T(8,128)S(1)}, u32[]{:S(2)}) copy-start(f32[6,1156]{1,0:T(8,128)S(1)} %copy.307) | copy-start | bytes 83236
  325.4 101.0 %copy-start.134 = (f32[6,1156]{1,0:T(8,128)}, f32[6,1156]{1,0:T(8,128)S(1)}, u32[]{:S(2)}) copy-start(f32[6,1156]{1,0:T(8,128)S(1)} %copy.310) | copy-start | bytes 83236
  325.7 100.8 %copy-start.135 = (f32[6,1156]{1,0:T(8,128)}, f32[6,1156]{1,0:T(8,128)S(1)}, u32[]{:S(2)}) copy-start(f32[6,1156]{1,0:T(8,128)S(1)} %copy.313) | copy-start | bytes 83236
  427.5 38.5 %copy-start.125 = (f32[6,1156]{1,0:T(8,128)}, f32[6,1156]{1,0:T(8,128)S(1)}, u32[]{:S(2)}) copy-start(f32[6,1156]{1,0:T(8,128)S(1)} %get-tuple-element.130) | copy-start | bytes 83236
  429.1 36.9 %copy-start.126 = (f32[6,1156]{1,0:T(8,128)}, f32[6,1156]{1,0:T(8,128)S(1)}, u32[]{:S(2)}) copy-start(f32[6,1156]{1,0:T(8,128)S(1)} %get-tuple-element.133) | copy-start | bytes 83236
  429.1 36.9 %copy-start.127 = (f32[6,1156]{1,0:T(8,128)}, f32[6,1156]{1,0:T(8,128)S(1)}, u32[]{:S(2)}) copy-start(f32[6,1156]{1,0:T(8,128)S(1)} %get-tuple-element.138) | copy-start | bytes 83236
  525.5 101.2 %collective-permute-start.6 = (bf16[768,34,1]{0,2,1:T(2,128)(2,1)S(1)}, bf16[768,34,1]{0,2,1:T(2,128)(2,1)S(1)}, u32[]{:S(2)}, u32[]{:S(2)}) collective-permute-start(bf16[768,34,1]{0,2,1:T(2,128)(2,1)S(1)} %get-tuple-element.84), channel_id=1, source_target_pairs={{0,14},{2,0},{4,2},{6,4},{8,6},{10,8},{12,10},{14,12},{1,15},{3,1}... | collective-permute-start | bytes 156680 | tf_op jit(solution)/shard_map/ppermute | solution.py:18
  525.8 101.0 %collective-permute-start.7 = (bf16[768,34,1]{0,2,1:T(2,128)(2,1)S(1)}, bf16[768,34,1]{0,2,1:T(2,128)(2,1)S(1)}, u32[]{:S(2)}, u32[]{:S(2)}) collective-permute-start(bf16[768,34,1]{0,2,1:T(2,128)(2,1)S(1)} %get-tuple-element.85), channel_id=1, source_target_pairs={{0,2},{2,4},{4,6},{6,8},{8,10},{10,12},{12,14},{14,0},{1,3},{3,5},... | collective-permute-start | bytes 156680 | tf_op jit(solution)/shard_map/ppermute | solution.py:18
  627.4 2.7 collective-permute-start.8
  636.3 182.4 %copy-start.7 = (f32[32,32,384]{2,1,0:T(8,128)}, f32[32,32,384]{2,1,0:T(8,128)S(1)}, u32[]{:S(2)}) copy-start(f32[32,32,384]{2,1,0:T(8,128)S(1)} %add_add_fusion.2) | copy-start | bytes 4718596
  667.4 144.6 %collective-permute-start.10 = (bf16[2,768,1024]{2,1,0:T(8,128)(2,1)}, bf16[2,768,1024]{2,1,0:T(8,128)(2,1)}, u32[]{:S(2)}, u32[]{:S(2)}) collective-permute-start(bf16[2,768,1024]{2,1,0:T(8,128)(2,1)} %get-tuple-element.65), channel_id=1, source_target_pairs={{0,2},{2,4},{4,6},{6,8},{8,10},{10,12},{12,14},{14,0},{1,3},{3,5},... | collective-permute-start | bytes 9437192 | tf_op jit(solution)/shard_map/ppermute | solution.py:18
  667.5 144.6 %collective-permute-start.9 = (bf16[2,768,1024]{2,1,0:T(8,128)(2,1)}, bf16[2,768,1024]{2,1,0:T(8,128)(2,1)}, u32[]{:S(2)}, u32[]{:S(2)}) collective-permute-start(bf16[2,768,1024]{2,1,0:T(8,128)(2,1)} %get-tuple-element.64), channel_id=1, source_target_pairs={{0,14},{2,0},{4,2},{6,4},{8,6},{10,8},{12,10},{14,12},{1,15},{3,1}... | collective-permute-start | bytes 9437192 | tf_op jit(solution)/shard_map/ppermute | solution.py:18
  818.7 8.4 collective-permute-start.11
  (167 other events, 683.8 us)
Sparse Core Ops, SparseCore 0:
  832.2 114.7 all-reduce.48
where the time goes:
time: 967 us; the launch traced here: 959 us
  local copies, waits for them, and re-layouts  465 us (48%)
  waiting for transfers between devices  192 us (20%)
  other arithmetic  190 us (20%)
  matrix products  46.3 us (5%)
  blocking collectives  30.4 us (3%)
  starting transfers between devices  18.9 us (2%)
  between operations  16.3 us (2%)
    ppermute x6, waiting for transfers between devices, passed_along(): return lax.ppermute(value, axis, pairs)  122 us
    mul x18, local copies, waits for them, and re-layouts, mix_heads(): result = result + (weight_one / weight_sum)[:, None, :] * value_one  84.1 us
    broadcast_in_dim x18, local copies, waits for them, and re-layouts, mix_heads(): jnp.sum(query_heads * key_one, axis=1) * head_size ** (-0.5)  83.7 us
    psum x1, waiting for transfers between devices, local(): lax.psum((jnp.stack([qkv_first, qkv_second]), jnp.stack([out_first, out_s...  66.4 us
    reshape x18, local copies, waits for them, and re-layouts, plain_mix(): key_list.append(window[:width].reshape(HEADS, head_size, points))  63.9 us
    reshape x18, local copies, waits for them, and re-layouts, plain_mix(): value_list.append(window[width:].reshape(HEADS, head_size, points))  59.8 us
    unnamed x365, local copies, waits for them, and re-layouts  39.3 us
    slice x10, local copies, waits for them, and re-layouts, plain_mix(): key_list.append(window[:width].reshape(HEADS, head_size, points))  35.1 us
  transfers between devices with their start and end apart: 13, of which 5 were waited for; matrix products, arithmetic and copies ran while one was open for 29% of the time, Pallas kernels for 0%

commit v1 on v0

--- a/solution.py
+++ b/solution.py
@@ -276,12 +276,15 @@
     )
     grad_tokens = jnp.where(shown, grad_start.reshape(row_count, col_count, width), 0.0)
     summed_qkv, summed_out, summed_gain = lax.psum(
-        (
-            jnp.stack([qkv_first, qkv_second]),
-            jnp.stack([out_first, out_second]),
-            jnp.stack([gain_first, gain_second]),
+        lax.psum(
+            (
+                jnp.stack([qkv_first, qkv_second]),
+                jnp.stack([out_first, out_second]),
+                jnp.stack([gain_first, gain_second]),
+            ),
+            "lat",
         ),
-        ("lon", "lat"),
+        "lon",
     )
     factor = (row_count * col_count * lat_count * lon_count) ** (-0.5)
     return (grad_tokens, summed_qkv * factor, summed_out * factor, summed_gain * factor)

time: 967 us -> 1050 us (1.086)
  waiting for transfers between devices: 192 us -> 285 us
    psum x0 -> x1, waiting for transfers between devices: none -> 133 us  [local(): lax.psum(lax.psum((jnp.stack([qkv_first, qkv_second]), jnp.stack([out_fir...]
    psum x1, waiting for transfers between devices: 66.4 us -> 26.6 us  [local(): lax.psum((jnp.stack([qkv_first, qkv_second]), jnp.stack([out_first, out_s...]
    psum x1, blocking collectives: 30.4 us -> 2.47 us  [local(): lax.psum((jnp.stack([qkv_first, qkv_second]), jnp.stack([out_first, out_s...]
    psum x0 -> x1, blocking collectives: none -> 22.5 us  [local(): lax.psum(lax.psum((jnp.stack([qkv_first, qkv_second]), jnp.stack([out_fir...]
  transfers between devices with their start and end apart: 13 -> 14, of which waited for: 5 -> 6; matrix products, arithmetic and copies ran while one was open for 29% -> 26% of each run, Pallas kernels for 0% -> 0%
where the time goes in v1:
time: 1050 us
  local copies, waits for them, and re-layouts  465 us (44%)
  waiting for transfers between devices  285 us (27%)
  other arithmetic  190 us (18%)
  matrix products  45.7 us (4%)
  blocking collectives  25 us (2%)
  starting transfers between devices  18.9 us (2%)
  between operations  16.3 us (2%)
    psum x1, waiting for transfers between devices, local(): lax.psum(lax.psum((jnp.stack([qkv_first, qkv_second]), jnp.stack([out_fir...  133 us
    ppermute x6, waiting for transfers between devices, passed_along(): return lax.ppermute(value, axis, pairs)  122 us
    mul x18, local copies, waits for them, and re-layouts, mix_heads(): result = result + (weight_one / weight_sum)[:, None, :] * value_one  84.2 us
    broadcast_in_dim x18, local copies, waits for them, and re-layouts, mix_heads(): jnp.sum(query_heads * key_one, axis=1) * head_size ** (-0.5)  83.8 us
    reshape x18, local copies, waits for them, and re-layouts, plain_mix(): key_list.append(window[:width].reshape(HEADS, head_size, points))  64 us
    reshape x18, local copies, waits for them, and re-layouts, plain_mix(): value_list.append(window[width:].reshape(HEADS, head_size, points))  59.8 us
    unnamed x365, local copies, waits for them, and re-layouts  39.3 us
    slice x10, local copies, waits for them, and re-layouts, plain_mix(): key_list.append(window[:width].reshape(HEADS, head_size, points))  35.3 us
  transfers between devices with their start and end apart: 14, of which 6 were waited for; matrix products, arithmetic and copies ran while one was open for 26% of the time, Pallas kernels for 0%

profile of v1, /device:TPU:0, one launch (start us, length us, event | category | flops | bytes accessed | tf_op | source)
XLA Modules:
  0.0 1046.6 jit_solution(14243752203043007502)
XLA Ops:
  43.2 119.3 %collective-permute-done.1 = bf16[2,768,1024]{2,1,0:T(8,128)(2,1)} collective-permute-done((bf16[2,768,1024]{2,1,0:T(8,128)(2,1)}, bf16[2,768,1024]{2,1,0:T(8,128)(2,1)}, u32[]{:S(2)}, u32[]{:S(2)}) %collective-permute-start.1) | collective-permute-done | bytes 3145760 | tf_op jit(solution)/shard_map/ppermute | solution.py:18
  169.9 6.6 fusion.90
  176.6 5.4 copy-done
  182.0 6.0 multiply_reduce_fusion.26
  213.7 10.3 fusion.92
  290.1 24.3 %multiply_reduce_fusion.17 = (f32[6,1156]{0,1:T(8,128)}, f32[6,1156]{0,1:T(8,128)S(1)}, f32[6,1156]{0,1:T(8,128)S(1)}, f32[6,1156]{0,1:T(8,128)}, f32[6,1156]{0,...) fusion(f32[6,64,1156]{1,0,2:T(8,128)} %reshape.1855, ...), kind=kLoop, calls=%fused_computation.21 | loop fusion | flops 7927848 | bytes 18005856 | tf_op jit(solution)/shard_map/transpose(jvp())/reduce_sum | solution.py:55
  391.5 24.1 %multiply_reduce_fusion.16 = (f32[6,1156]{0,1:T(8,128)}, f32[6,1156]{0,1:T(8,128)S(1)}, f32[6,1156]{0,1:T(8,128)S(1)}, f32[6,1156]{0,1:T(8,128)}, f32[6,1156]{0,...) fusion(f32[6,64,1156]{1,0,2:T(8,128)} %reshape.1864, ...), kind=kLoop, calls=%fused_computation.20 | loop fusion | flops 7927848 | bytes 18005856 | tf_op jit(solution)/shard_map/jvp()/reduce_sum | solution.py:48
  466.2 5.6 bitcast_multiply_fusion.29
  493.2 9.4 pad_add_fusion.13
  502.6 10.4 pad_add_fusion.1
  513.0 5.3 copy.367
  569.1 5.2 broadcast_in_dim.190
  606.4 5.2 broadcast_in_dim.198
  642.7 9.2 bitcast_multiply_fusion.10
  651.9 12.2 %fusion.89 = (bf16[6,768,1024]{2,1,0:T(8,128)(2,1)S(1)}, f32[6,768,1024]{2,1,0:T(8,128)}) fusion(f32[1,384,1024]{2,1,0:T(8,128)} %bitcast.394, f32[1,384,1024]{2,1,0:T(8,128)} %bitcast.395, f32[1,384,1024]{2,1,0:T(8,128)} %bitcast.396, f32[1,384,1024]{2,1,0:T(8,128)} %bitcast.397, f32[1,384,1024]{2,1,0:T(8,128)} %bitcast.398, ...), kind=kLoop, calls=%fused_computation.278 | loop fusion | flops 56623104 | bytes 47185920 | tf_op jit(solution)/shard_map/convert.12
  736.7 5.2 mul.2015
  764.5 5.2 mul.2023
  783.0 5.6 mul.2027
  801.2 9.7 convolution_bitcast_fusion.1
  812.3 6.3 fusion
  832.3 26.6 %all-reduce.53.cloned.1.call-done = (f32[2,384,1152]{2,1,0:T(8,128)}, f32[2,384,384]{2,1,0:T(8,128)}) async-done(((f32[2,384,1152]{2,1,0:T(8,128)}, f32[2,384,384]{2,1,0:T(8,128)}), (f32[2,384,1152]{2,1,0:T(8,128)}, f32[2,384,384]{2,1,0:T(8,128)})) %all-reduce.53.cloned.1.call-update) | async-done | bytes 4718608 | tf_op jit(solution)/shard_map/psum | solution.py:279
  860.1 7.1 fusion.5
  875.4 22.5 %psum.47 = f32[2,384]{1,0:T(2,128)S(1)} all-reduce(f32[2,384]{1,0:T(2,128)S(1)} %psum.46), channel_id=1, replica_groups=mesh['group'=2,'lon'=8,'lat'=2] {'lon'}, use_global_device_ids=true, to_apply=%region_45.46 | all-reduce | flops 768 | bytes 6144 | tf_op jit(solution)/shard_map/psum | solution.py:278
  901.4 133.0 %all-reduce.51.cloned.1.call-done = (f32[2,384,1152]{2,1,0:T(8,128)}, f32[2,384,384]{2,1,0:T(8,128)}) async-done(((f32[2,384,1152]{2,1,0:T(8,128)}, f32[2,384,384]{2,1,0:T(8,128)}), (f32[2,384,1152]{2,1,0:T(8,128)}, f32[2,384,384]{2,1,0:T(8,128)})) %all-reduce.51.cloned.1.call-update) | async-done | bytes 4718608 | tf_op jit(solution)/shard_map/psum | solution.py:278
  (607 shorter events, 550.8 us)
Async XLA Ops:
  7.2 851.7 %all-reduce.53.cloned.1.call-start = ((), (), s32[]{:S(2)}) async-start(), calls=%async_computation.1 | async-start | bytes 9437184 | tf_op jit(solution)/shard_map/psum | solution.py:279
  13.3 178.7 %copy-start.176 = (f32[384]{0:T(512)}, f32[384]{0:T(512)S(1)}, u32[]{:S(2)}) copy-start(f32[384]{0:T(512)S(1)} %get-tuple-element.38) | copy-start | bytes 4612
  18.3 3.6 collective-permute-start
  24.2 138.3 %collective-permute-start.1 = (bf16[2,768,1024]{2,1,0:T(8,128)(2,1)}, bf16[2,768,1024]{2,1,0:T(8,128)(2,1)}, u32[]{:S(2)}, u32[]{:S(2)}) collective-permute-start(bf16[2,768,1024]{2,1,0:T(8,128)(2,1)} %pad_maximum_fusion.1), channel_id=1, source_target_pairs={{0,2},{2,4},{4,6},{6,8},{8,10},{10,12},{12,14},{14,0},{1,3},{3,5},... | collective-permute-start | bytes 9437192 | tf_op jit(solution)/shard_map/ppermute | solution.py:18
  27.1 138.0 %collective-permute-start.2 = (bf16[2,768,1024]{2,1,0:T(8,128)(2,1)}, bf16[2,768,1024]{2,1,0:T(8,128)(2,1)}, u32[]{:S(2)}, u32[]{:S(2)}) collective-permute-start(bf16[2,768,1024]{2,1,0:T(8,128)(2,1)} %pad_maximum_fusion.1), channel_id=1, source_target_pairs={{0,14},{2,0},{4,2},{6,4},{8,6},{10,8},{12,10},{14,12},{1,15},{3,1}... | collective-permute-start | bytes 9437192 | tf_op jit(solution)/shard_map/ppermute | solution.py:18
  193.6 1.3 collective-permute-start.3
  195.4 12.1 %collective-permute-start.4 = (bf16[768,34,1]{0,2,1:T(2,128)(2,1)S(1)}, bf16[768,34,1]{0,2,1:T(2,128)(2,1)S(1)}, u32[]{:S(2)}, u32[]{:S(2)}) collective-permute-start(bf16[768,34,1]{0,2,1:T(2,128)(2,1)S(1)} %get-tuple-element.108), channel_id=1, source_target_pairs={{0,2},{2,4},{4,6},{6,8},{8,10},{10,12},{12,14},{14,0},{1,3},{3,5},... | collective-permute-start | bytes 156680 | tf_op jit(solution)/shard_map/ppermute | solution.py:28
  195.4 12.0 %collective-permute-start.5 = (bf16[768,34,1]{0,2,1:T(2,128)(2,1)S(1)}, bf16[768,34,1]{0,2,1:T(2,128)(2,1)S(1)}, u32[]{:S(2)}, u32[]{:S(2)}) collective-permute-start(bf16[768,34,1]{0,2,1:T(2,128)(2,1)S(1)} %get-tuple-element.109), channel_id=1, source_target_pairs={{2,0},{4,2},{6,4},{8,6},{10,8},{12,10},{14,12},{0,14},{3,1},{5,3},... | collective-permute-start | bytes 156680 | tf_op jit(solution)/shard_map/ppermute | solution.py:30
  317.6 109.0 %copy-start.131 = (f32[6,1156]{1,0:T(8,128)}, f32[6,1156]{1,0:T(8,128)S(1)}, u32[]{:S(2)}) copy-start(f32[6,1156]{1,0:T(8,128)S(1)} %copy.292) | copy-start | bytes 83236
  318.9 107.7 %copy-start.132 = (f32[6,1156]{1,0:T(8,128)}, f32[6,1156]{1,0:T(8,128)S(1)}, u32[]{:S(2)}) copy-start(f32[6,1156]{1,0:T(8,128)S(1)} %copy.295) | copy-start | bytes 83236
  325.3 101.3 %copy-start.133 = (f32[6,1156]{1,0:T(8,128)}, f32[6,1156]{1,0:T(8,128)S(1)}, u32[]{:S(2)}) copy-start(f32[6,1156]{1,0:T(8,128)S(1)} %copy.307) | copy-start | bytes 83236
  325.5 101.0 %copy-start.134 = (f32[6,1156]{1,0:T(8,128)}, f32[6,1156]{1,0:T(8,128)S(1)}, u32[]{:S(2)}) copy-start(f32[6,1156]{1,0:T(8,128)S(1)} %copy.310) | copy-start | bytes 83236
  325.8 100.8 %copy-start.135 = (f32[6,1156]{1,0:T(8,128)}, f32[6,1156]{1,0:T(8,128)S(1)}, u32[]{:S(2)}) copy-start(f32[6,1156]{1,0:T(8,128)S(1)} %copy.313) | copy-start | bytes 83236
  427.7 38.5 %copy-start.125 = (f32[6,1156]{1,0:T(8,128)}, f32[6,1156]{1,0:T(8,128)S(1)}, u32[]{:S(2)}) copy-start(f32[6,1156]{1,0:T(8,128)S(1)} %get-tuple-element.132) | copy-start | bytes 83236
  429.2 36.9 %copy-start.126 = (f32[6,1156]{1,0:T(8,128)}, f32[6,1156]{1,0:T(8,128)S(1)}, u32[]{:S(2)}) copy-start(f32[6,1156]{1,0:T(8,128)S(1)} %get-tuple-element.135) | copy-start | bytes 83236
  429.2 36.9 %copy-start.127 = (f32[6,1156]{1,0:T(8,128)}, f32[6,1156]{1,0:T(8,128)S(1)}, u32[]{:S(2)}) copy-start(f32[6,1156]{1,0:T(8,128)S(1)} %get-tuple-element.140) | copy-start | bytes 83236
  525.7 101.2 %collective-permute-start.6 = (bf16[768,34,1]{0,2,1:T(2,128)(2,1)S(1)}, bf16[768,34,1]{0,2,1:T(2,128)(2,1)S(1)}, u32[]{:S(2)}, u32[]{:S(2)}) collective-permute-start(bf16[768,34,1]{0,2,1:T(2,128)(2,1)S(1)} %get-tuple-element.86), channel_id=1, source_target_pairs={{0,14},{2,0},{4,2},{6,4},{8,6},{10,8},{12,10},{14,12},{1,15},{3,1}... | collective-permute-start | bytes 156680 | tf_op jit(solution)/shard_map/ppermute | solution.py:18
  526.0 101.0 %collective-permute-start.7 = (bf16[768,34,1]{0,2,1:T(2,128)(2,1)S(1)}, bf16[768,34,1]{0,2,1:T(2,128)(2,1)S(1)}, u32[]{:S(2)}, u32[]{:S(2)}) collective-permute-start(bf16[768,34,1]{0,2,1:T(2,128)(2,1)S(1)} %get-tuple-element.87), channel_id=1, source_target_pairs={{0,2},{2,4},{4,6},{6,8},{8,10},{10,12},{12,14},{14,0},{1,3},{3,5},... | collective-permute-start | bytes 156680 | tf_op jit(solution)/shard_map/ppermute | solution.py:18
  627.6 2.7 collective-permute-start.8
  636.5 182.4 %copy-start.7 = (f32[32,32,384]{2,1,0:T(8,128)}, f32[32,32,384]{2,1,0:T(8,128)S(1)}, u32[]{:S(2)}) copy-start(f32[32,32,384]{2,1,0:T(8,128)S(1)} %add_add_fusion.2) | copy-start | bytes 4718596
  667.6 144.7 %collective-permute-start.10 = (bf16[2,768,1024]{2,1,0:T(8,128)(2,1)}, bf16[2,768,1024]{2,1,0:T(8,128)(2,1)}, u32[]{:S(2)}, u32[]{:S(2)}) collective-permute-start(bf16[2,768,1024]{2,1,0:T(8,128)(2,1)} %get-tuple-element.67), channel_id=1, source_target_pairs={{0,2},{2,4},{4,6},{6,8},{8,10},{10,12},{12,14},{14,0},{1,3},{3,5},... | collective-permute-start | bytes 9437192 | tf_op jit(solution)/shard_map/ppermute | solution.py:18
  667.6 144.7 %collective-permute-start.9 = (bf16[2,768,1024]{2,1,0:T(8,128)(2,1)}, bf16[2,768,1024]{2,1,0:T(8,128)(2,1)}, u32[]{:S(2)}, u32[]{:S(2)}) collective-permute-start(bf16[2,768,1024]{2,1,0:T(8,128)(2,1)} %get-tuple-element.66), channel_id=1, source_target_pairs={{0,14},{2,0},{4,2},{6,4},{8,6},{10,8},{12,10},{14,12},{1,15},{3,1}... | collective-permute-start | bytes 9437192 | tf_op jit(solution)/shard_map/ppermute | solution.py:18
  818.9 8.4 collective-permute-start.11
  832.3 202.1 %all-reduce.51.cloned.1.call-start = ((), (), s32[]{:S(2)}) async-start(), calls=%async_computation | async-start | bytes 9437184 | tf_op jit(solution)/shard_map/psum | solution.py:278
  (168 other events, 704.6 us)
Sparse Core Ops, SparseCore 0:
  832.4 26.4 all-reduce.52
  862.9 171.3 all-reduce.50
